TPU v7x, 128 devices: a whole 4x4x4 slice. The times are simulated.
128 devices in a mesh: ctx: 16 (over y, x_hi, core), tp: 8 (over x_lo, z).
Axes of the slice: x: 4 (x_hi: 2, x_lo: 2; x = x_hi * 2 + x_lo), y: 4, z: 4, core: 2. Of those that a mesh axis runs over, the one named last changes fastest.
Arguments:
- hyena_query: bfloat16 [6144, 8192], P('ctx', 'tp'), may hold values from -6 to 6
- hyena_key: bfloat16 [6144, 8192], P('ctx', 'tp'), may hold values from -6 to 6
- hyena_value: bfloat16 [6144, 8192], P('ctx', 'tp'), may hold values from -6 to 6
- conv_filter: bfloat16 [512, 128], P('tp'), may hold values from -0.5 to 0.5
- skip_gain: float32 [8192], P('tp'), may hold values from -4 to 4
- query_rows: bfloat16 [6144, 8192], P('ctx', 'tp'), may hold values from -80 to 80
- key_rows: bfloat16 [6144, 8192], P('ctx', 'tp'), may hold values from -4 to 4, as said below
- value_rows: bfloat16 [6144, 8192], P('ctx', 'tp'), may hold values from -6 to 6
- out_weight: bfloat16 [8192, 8192], P(None, 'tp'), may hold values from -1 to 1
Outputs:
- hyena_out: bfloat16 [6144, 8192], P('ctx', 'tp')
- attention_out: bfloat16 [8192, 6144], P('tp', 'ctx')
Inputs may be any that keep to these rules, and one draw needn't show every extreme that they name: `key_rows`: keys of order one.
All inputs are finite; a program needn't handle non-finite values.
Results may differ from a plain program's by a relative error of at most 0.014.
Values may be sent and summed in bfloat16 or wider, within the bound.
No kernel may reach another device: no remote copies, remote signals or barrier semaphores. Data moves between devices by JAX's collectives and lax.ppermute only.
A program may use at most 128 MiB of HBM per device.

v0:
```python
import jax
import jax.numpy as jnp
from jax import lax
from jax.sharding import PartitionSpec as P

HEAD_DIM = 128


def shifted(block, axis, distance):
    devices = range(lax.axis_size(axis))
    route = [(i - distance, i) for i in devices if i - distance in devices]
    return lax.ppermute(block, axis, route)


def toeplitz_pair(filters):
    length = filters.shape[1]
    lag_table = (
        jnp.arange(length, dtype=jnp.int32)[:, None] - jnp.arange(length, dtype=jnp.int32)[None, :]
    )
    taps = jnp.arange(length, dtype=jnp.int32)[:, None, None]
    inner_table = (lag_table[None] == taps).astype(jnp.bfloat16)
    outer_table = (lag_table[None] + length == taps).astype(jnp.bfloat16)
    inner_part = jnp.einsum(
        "gj,jts->gts", filters, inner_table, preferred_element_type=jnp.float32
    ).astype(jnp.bfloat16)
    outer_part = jnp.einsum(
        "gj,jts->gts", filters, outer_table, preferred_element_type=jnp.float32
    ).astype(jnp.bfloat16)
    return (inner_part, outer_part)


def local_conv(current, before, filters):
    blocks, length, feature_width = current.shape
    groups = filters.shape[0]
    split_shape = (blocks, length, groups, feature_width // groups)
    inner_part, outer_part = toeplitz_pair(filters)
    result = jnp.einsum(
        "gts,bsgc->btgc",
        inner_part,
        current.reshape(split_shape),
        preferred_element_type=jnp.float32,
    )
    result = result + jnp.einsum(
        "gts,bsgc->btgc",
        outer_part,
        before.reshape(split_shape),
        preferred_element_type=jnp.float32,
    )
    return result.reshape(blocks * length, feature_width)


def half_update(partial_value, block_keys, block_values, block_first, queries, positions):
    row_top, row_total, weighted = partial_value
    score_scale = HEAD_DIM ** (-0.5)
    scores = (
        jnp.einsum("qhd,khd->hqk", queries, block_keys, preferred_element_type=jnp.float32)
        * score_scale
    )
    key_positions = block_first + jnp.arange(block_keys.shape[0], dtype=jnp.int32)
    allowed = key_positions[None, :] <= positions[:, None]
    scores = jnp.where(allowed[None], scores, -jnp.inf)
    new_top = jnp.maximum(row_top, jnp.max(scores, axis=2))
    safe_top = jnp.where(new_top == -jnp.inf, 0.0, new_top)
    keep_factor = jnp.exp(row_top - safe_top)
    weights = jnp.exp(scores - safe_top[:, :, None])
    row_total = row_total * keep_factor + jnp.sum(weights, axis=2)
    weighted = weighted * keep_factor[:, :, None] + jnp.einsum(
        "hqk,khd->hqd",
        weights.astype(jnp.bfloat16),
        block_values,
        preferred_element_type=jnp.float32,
    )
    return (new_top, row_total, weighted)


def local(
    hyena_query,
    hyena_key,
    hyena_value,
    conv_filter,
    skip_gain,
    query_rows,
    key_rows,
    value_rows,
    out_weight,
):
    product = (hyena_key.astype(jnp.float32) * hyena_value.astype(jnp.float32)).astype(jnp.bfloat16)
    length = conv_filter.shape[1]
    tokens_here, feature_width = product.shape
    blocks = tokens_here // length
    previous = shifted(product[tokens_here - length :], "ctx", 1)
    widened = product.astype(jnp.float32)
    earlier = jnp.concatenate([previous, product[: tokens_here - length]], axis=0)
    convolved = local_conv(
        product.reshape(blocks, length, feature_width),
        earlier.reshape(blocks, length, feature_width),
        conv_filter,
    )
    hyena_out = (
        hyena_query.astype(jnp.float32) * (convolved + skip_gain[None, :] * widened)
    ).astype(jnp.bfloat16)
    ctx_index = lax.axis_index("ctx")
    half_rows = tokens_here // 2
    heads_here = feature_width // HEAD_DIM
    offsets = jnp.arange(half_rows, dtype=jnp.int32)
    first_positions = ctx_index * tokens_here + offsets
    second_queries = query_rows[half_rows:]
    second_positions = ctx_index * tokens_here + half_rows + offsets
    query_halves = (
        query_rows[:half_rows].reshape(half_rows, heads_here, HEAD_DIM),
        second_queries.reshape(half_rows, heads_here, HEAD_DIM),
    )
    position_halves = (first_positions, second_positions)
    empty_top = jnp.full((heads_here, half_rows), -jnp.inf, jnp.float32)
    empty_total = jnp.zeros((heads_here, half_rows), jnp.float32)
    empty_weighted = jnp.zeros((heads_here, half_rows, HEAD_DIM), jnp.float32)
    start_state = (
        (empty_top, empty_total, empty_weighted),
        (empty_top, empty_total, empty_weighted),
    )
    key_piece = lax.all_gather(key_rows, "ctx", axis=0, tiled=True)
    value_piece = lax.all_gather(value_rows, "ctx", axis=0, tiled=True)
    piece_rows = key_piece.shape[0]
    step_rows = min(piece_rows, tokens_here)
    count_steps = piece_rows // step_rows
    key_steps = key_piece.reshape(count_steps, step_rows, heads_here, HEAD_DIM)
    value_steps = value_piece.reshape(count_steps, step_rows, heads_here, HEAD_DIM)

    def one_step(carried, inputs):
        block_keys, block_values, step_index = inputs
        block_first = step_index * step_rows
        updated = []
        for half_index in range(2):
            queries = query_halves[half_index]
            positions = position_halves[half_index]

            def apply_update(partial_value, queries=queries, positions=positions):
                return half_update(
                    partial_value, block_keys, block_values, block_first, queries, positions
                )

            def leave_alone(partial_value):
                return partial_value

            updated.append(
                lax.cond(
                    block_first <= positions[half_rows - 1],
                    apply_update,
                    leave_alone,
                    carried[half_index],
                )
            )
        return ((updated[0], updated[1]), None)

    final_state, unused = lax.scan(
        one_step, start_state, (key_steps, value_steps, jnp.arange(count_steps, dtype=jnp.int32))
    )
    first_state, second_state = final_state

    def finish(partial_value):
        row_top, row_total, weighted = partial_value
        normalized = weighted / row_total[:, :, None]
        return (
            jnp.transpose(normalized, (1, 0, 2))
            .reshape(half_rows, feature_width)
            .astype(jnp.bfloat16)
        )

    first_result = finish(first_state)
    second_result = finish(second_state)
    attended = jnp.concatenate([first_result, second_result], axis=0)
    attention_out = lax.psum_scatter(
        lax.dot_general(
            out_weight, attended, (((1,), (1,)), ((), ())), preferred_element_type=jnp.float32
        ).astype(jnp.bfloat16),
        "tp",
        scatter_dimension=0,
        tiled=True,
    )
    return (hyena_out, attention_out)


def solution(mesh):
    in_specs = (
        P("ctx", "tp"),
        P("ctx", "tp"),
        P("ctx", "tp"),
        P("tp", None),
        P("tp"),
        P("ctx", "tp"),
        P("ctx", "tp"),
        P("ctx", "tp"),
        P(None, "tp"),
    )
    out_specs = (P("ctx", "tp"), P("tp", "ctx"))
    return jax.shard_map(local, mesh=mesh, in_specs=in_specs, out_specs=out_specs, check_vma=False)
```

profile of v0, /device:TPU:1, one launch (start us, length us, event | category | flops | bytes accessed | tf_op | source)
XLA Modules:
  0.0 493.8 jit_solution(8231100119584761282)
XLA Ops:
  7.2 0.7 all-gather.3.cloned.1.call-update
  8.0 0.7 all-gather.5.cloned.1.call-update
  8.7 1.2 slice_bitcast_fusion
  10.1 94.3 %all-gather.3.cloned.1.call-done = bf16[6144,1024]{1,0:T(8,128)(2,1)} async-done(((bf16[384,1024]{1,0:T(8,128)(2,1)}), bf16[6144,1024]{1,0:T(8,128)(2,1)}) %all-gather.3.cloned.1.call-update) | async-done | bytes 12582928 | tf_op jit(solution)/shard_map/all_gather | solution.py:121
  104.4 12.0 %copy.40 = bf16[768,8,8,128]{3,2,1,0:T(8,128)(2,1)} copy(bf16[768,8,8,128]{3,1,2,0:T(8,128)(2,1)} %bitcast.97) | data formatting | bytes 25165824
  116.4 78.6 %all-gather.5.cloned.1.call-done = bf16[6144,1024]{1,0:T(8,128)(2,1)} async-done(((bf16[384,1024]{1,0:T(8,128)(2,1)}), bf16[6144,1024]{1,0:T(8,128)(2,1)}) %all-gather.5.cloned.1.call-update) | async-done | bytes 12582928 | tf_op jit(solution)/shard_map/all_gather | solution.py:122
  195.0 11.9 %copy.41 = bf16[768,8,8,128]{3,2,1,0:T(8,128)(2,1)} copy(bf16[768,8,8,128]{3,1,2,0:T(8,128)(2,1)} %bitcast.98) | data formatting | bytes 25165824
  207.0 0.9 broadcast_in_dim.52
  207.9 103.0 %while.20 = (s32[]{:T(128)}, f32[8,192]{1,0:T(8,128)S(1)}, f32[8,192]{1,0:T(8,128)S(1)}, f32[8,192,128]{2,1,0:T(8,128)}, f32[8,192]{1,0:T(8,128)S(1)}, /*index=5...) while((s32[]{:T(128)}, f32[8,192]{1,0:T(8,128)S(1)}, ...), condition=%wide.region_9.10_spmd, body=%wide.region_0.9_spmd.sunk | while | flops 617908992 | bytes 34623508 | solution.py:155
  208.5 0.7 slice.29
  211.8 1.5 constant_dynamic-slice_fusion.3
  213.5 3.7 conditional.4
  214.3 0.9 fusion.2
  215.2 1.1 convolution_add_fusion
  216.3 0.9 copy-done.5
  217.2 2.8 conditional.5
  217.9 0.9 fusion.12
  218.9 1.1 convolution_add_fusion.1
  220.6 0.7 slice.29
  223.8 1.5 constant_dynamic-slice_fusion.3
  225.6 3.7 conditional.4
  226.3 0.9 fusion.2
  227.3 1.1 convolution_add_fusion
  228.4 0.9 copy-done.5
  229.3 2.8 conditional.5
  230.0 0.9 fusion.12
  230.9 1.1 convolution_add_fusion.1
  235.9 1.5 constant_dynamic-slice_fusion.3
  238.3 0.7 slice.29
  241.6 1.5 constant_dynamic-slice_fusion.3
  243.9 0.7 slice.29
  247.2 1.5 constant_dynamic-slice_fusion.3
  249.6 0.7 slice.29
  252.8 1.5 constant_dynamic-slice_fusion.3
  258.5 1.5 constant_dynamic-slice_fusion.3
  264.1 1.5 constant_dynamic-slice_fusion.3
  269.7 1.5 constant_dynamic-slice_fusion.3
  275.4 1.5 constant_dynamic-slice_fusion.3
  281.0 1.5 constant_dynamic-slice_fusion.3
  286.6 1.5 constant_dynamic-slice_fusion.3
  289.0 0.7 slice.29
  292.3 1.5 constant_dynamic-slice_fusion.3
  294.6 0.7 slice.29
  297.9 1.5 constant_dynamic-slice_fusion.3
  300.3 0.7 slice.29
  303.5 1.5 constant_dynamic-slice_fusion.3
  309.2 1.5 constant_dynamic-slice_fusion.3
  311.2 1.4 copy_bitcast_fusion.3
  312.6 12.0 %fusion.20 = bf16[8192,384]{0,1:T(8,128)(2,1)} fusion(bf16[8192,1024]{1,0:T(8,128)(2,1)} %param.23, bf16[192,1024]{1,0:T(8,128)(2,1)S(1)} %copy_bitcast_fusion.2, bf16[192,1024]{1,0:T(8,128)(2,1)S(1)} %copy_bitcast_fusion.3), kind=kOutput, calls=%fused_computation.39 | convolution fusion | flops 6447169536 | bytes 23855104 | tf_op jit(solution)/shard_map/dot_general | solution.py:173
  324.7 1.1 copy-done.6
  326.8 9.1 %collective-permute-start = (bf16[128,1024]{0,1:T(8,128)(2,1)S(1)}, bf16[128,1024]{0,1:T(8,128)(2,1)}, u32[]{:S(2)}, u32[]{:S(2)}) collective-permute-start(bf16[128,1024]{0,1:T(8,128)(2,1)S(1)} %slice.22), channel_id=1, source_target_pairs={{0,8},{8,16},{16,24},{24,32},{32,40},{40,48},{48,56},{56,64},{64,7... | collective-permute-start | bytes 786440 | tf_op jit(solution)/shard_map/ppermute | solution.py:12
  336.2 1.1 copy.13
  337.3 1.2 iota_compare_fusion.1
  338.6 3.4 fusion.23
  342.0 2.3 fusion.26
  344.2 1.3 iota_compare_fusion
  345.5 4.7 fusion.21
  350.3 1.9 pad_maximum_fusion
  352.2 2.6 reshape_reshape.7
  354.8 4.0 add_bitcast_fusion
  358.8 0.9 copy.18
  360.5 1.2 copy.25
  361.7 123.3 %reduce-scatter.2.cloned.1.call-done = bf16[1024,384]{0,1:T(8,128)(2,1)} async-done(((bf16[8192,384]{0,1:T(8,128)(2,1)}), bf16[1024,384]{0,1:T(8,128)(2,1)}) %reduce-scatter.2.cloned.1.call-update) | async-done | bytes 786448 | tf_op jit(solution)/shard_map/reduce_scatter | solution.py:172
  485.0 2.3 copy.26
  (169 shorter events, 34.8 us)
Async XLA Ops:
  7.2 331.4 %copy-start = (bf16[64,128]{1,0:T(8,128)(2,1)S(1)}, bf16[64,128]{1,0:T(8,128)(2,1)}, u32[]{:S(2)}) copy-start(bf16[64,128]{1,0:T(8,128)(2,1)} %param.18) | copy-start | bytes 49156
  7.2 97.2 %all-gather.3.cloned.1.call-start = ((), (), s32[]{:S(2)}) async-start(), calls=%async_computation.1 | async-start | bytes 13369344 | tf_op jit(solution)/shard_map/all_gather | solution.py:121
  7.9 187.1 %all-gather.5.cloned.1.call-start = ((), (), s32[]{:S(2)}) async-start(), calls=%async_computation.2 | async-start | bytes 13369344 | tf_op jit(solution)/shard_map/all_gather | solution.py:122
  8.7 476.3 %reduce-scatter.2.cloned.1.call-start = ((), (), s32[]{:S(2)}) async-start(), calls=%async_computation.3 | async-start | bytes 7077888 | tf_op jit(solution)/shard_map/reduce_scatter | solution.py:172
  213.6 1.6 copy-start.4
  216.3 0.9 copy-start.5
  225.7 1.6 copy-start.4
  228.4 0.9 copy-start.5
  324.7 1.1 copy-start.6
  324.7 1.5 copy-start.7
  326.7 10.6 %copy-start.1 = (bf16[384,1024]{0,1:T(8,128)(2,1)}, bf16[384,1024]{0,1:T(8,128)(2,1)S(1)}, u32[]{:S(2)}) copy-start(bf16[384,1024]{0,1:T(8,128)(2,1)S(1)} %multiply_convert_fusion) | copy-start | bytes 2359300
  326.8 9.4 %copy-start.8 = (bf16[384,1024]{1,0:T(8,128)(2,1)S(1)}, bf16[384,1024]{1,0:T(8,128)(2,1)}, u32[]{:S(2)}) copy-start(bf16[384,1024]{1,0:T(8,128)(2,1)} %param.15) | copy-start | bytes 2359300
  326.8 23.5 %collective-permute-start = (bf16[128,1024]{0,1:T(8,128)(2,1)S(1)}, bf16[128,1024]{0,1:T(8,128)(2,1)}, u32[]{:S(2)}, u32[]{:S(2)}) collective-permute-start(bf16[128,1024]{0,1:T(8,128)(2,1)S(1)} %slice.22), channel_id=1, source_target_pairs={{0,8},{8,16},{16,24},{24,32},{32,40},{40,48},{48,56},{56,64},{64,7... | collective-permute-start | bytes 786440 | tf_op jit(solution)/shard_map/ppermute | solution.py:12
  345.5 4.7 slice-start
  358.8 1.1 copy-start.2
  358.8 1.4 copy-start.3
  358.8 1.4 copy-start.9
Sparse Core Ops, SparseCore 0:
  10.4 93.9 all-gather.2
  106.9 88.0 all-gather.4
  324.8 160.1 reduce-scatter.1
where the time goes:
time: 495 us; the launch traced here: 494 us
  waiting for transfers between devices  298 us (60%)
  local copies, waits for them, and re-layouts  96.2 us (19%)
  matrix products  33.3 us (7%)
  loops' own time  32.8 us (7%)
  between operations  14 us (3%)
  other arithmetic  10.8 us (2%)
  starting transfers between devices  9.21 us (2%)
    reduce_scatter x1, waiting for transfers between devices, local(): lax.psum_scatter(lax.dot_general(out_weight, attended, (((1,), (1,)), (()...  123 us
    all_gather x1, waiting for transfers between devices, local(): key_piece = lax.all_gather(key_rows, 'ctx', axis=0, tiled=True)  94.3 us
    all_gather x1, waiting for transfers between devices, local(): value_piece = lax.all_gather(value_rows, 'ctx', axis=0, tiled=True)  78.6 us
    dynamic_slice x64, local copies, waits for them, and re-layouts, local(): lax.scan(one_step, start_state, (key_steps, value_steps, jnp.arange(count...  37.4 us
    another operation x1, loops' own time, local(): lax.scan(one_step, start_state, (key_steps, value_steps, jnp.arange(count...  32 us
    unnamed x24, local copies, waits for them, and re-layouts  32 us
    slice x32, local copies, waits for them, and re-layouts, one_step(): positions[half_rows - 1]  20.1 us
    dot_general x1, matrix products, local(): lax.dot_general(out_weight, attended, (((1,), (1,)), ((), ())), preferred...  12 us
  transfers between devices with their start and end apart: 4, of which 3 were waited for; matrix products, arithmetic and copies ran while one was open for 8% of the time, Pallas kernels for 0%

commit v1 on v0

--- a/solution.py
+++ b/solution.py
@@ -118,7 +118,10 @@
         (empty_top, empty_total, empty_weighted),
         (empty_top, empty_total, empty_weighted),
     )
-    key_piece = lax.all_gather(key_rows, "ctx", axis=0, tiled=True)
+    peers = lax.axis_size("ctx")
+    parts = jnp.stack([key_rows for _ in range(peers)])
+    parts = lax.all_to_all(parts, "ctx", split_axis=0, concat_axis=0)
+    key_piece = jnp.concatenate(parts, axis=0)
     value_piece = lax.all_gather(value_rows, "ctx", axis=0, tiled=True)
     piece_rows = key_piece.shape[0]
     step_rows = min(piece_rows, tokens_here)

time: 495 us -> 537 us (1.085)
  waiting for transfers between devices: 298 us -> 322 us
  local copies, waits for them, and re-layouts: 96.2 us -> 108 us
  starting transfers between devices: 9.21 us -> 16.9 us
    all_gather x1, waiting for transfers between devices: 78.6 us -> 197 us  [local(): value_piece = lax.all_gather(value_rows, 'ctx', axis=0, tiled=True)]
    all_gather x1 -> x0, waiting for transfers between devices: 94.3 us -> none  [local(): key_piece = lax.all_gather(key_rows, 'ctx', axis=0, tiled=True)]
    dynamic_slice x64 -> x80, local copies, waits for them, and re-layouts: 37.4 us -> 56.1 us  [local(): lax.scan(one_step, start_state, (key_steps, value_steps, jnp.arange(count...]
    unnamed x24 -> x26, local copies, waits for them, and re-layouts: 32 us -> 20.4 us
    all_to_all x0 -> x1, starting transfers between devices: none -> 8.57 us  [local(): parts = lax.all_to_all(parts, 'ctx', split_axis=0, concat_axis=0)]
    another operation x2 -> x3, local copies, waits for them, and re-layouts: 0.01 us -> 6.1 us  [the longest x1 6.09 us: local(): parts = jnp.stack([key_rows for _ in range(peers)])]
  transfers between devices with their start and end apart: 4 -> 4, of which waited for: 3 -> 2; matrix products, arithmetic and copies ran while one was open for 8% -> 9% of each run, Pallas kernels for 0% -> 0%
where the time goes in v1:
time: 537 us; the launch traced here: 535 us
  waiting for transfers between devices  322 us (60%)
  local copies, waits for them, and re-layouts  108 us (20%)
  matrix products  33.2 us (6%)
  loops' own time  29.8 us (6%)
  starting transfers between devices  16.9 us (3%)
  between operations  14.3 us (3%)
  other arithmetic  10.8 us (2%)
    all_gather x1, waiting for transfers between devices, local(): value_piece = lax.all_gather(value_rows, 'ctx', axis=0, tiled=True)  197 us
    reduce_scatter x1, waiting for transfers between devices, local(): lax.psum_scatter(lax.dot_general(out_weight, attended, (((1,), (1,)), (()...  123 us
    dynamic_slice x80, local copies, waits for them, and re-layouts, local(): lax.scan(one_step, start_state, (key_steps, value_steps, jnp.arange(count...  56.1 us
    another operation x1, loops' own time, local(): lax.scan(one_step, start_state, (key_steps, value_steps, jnp.arange(count...  29.1 us
    unnamed x26, local copies, waits for them, and re-layouts  20.4 us
    slice x32, local copies, waits for them, and re-layouts, one_step(): positions[half_rows - 1]  18.4 us
    dot_general x1, matrix products, local(): lax.dot_general(out_weight, attended, (((1,), (1,)), ((), ())), preferred...  12 us
  transfers between devices with their start and end apart: 4, of which 2 were waited for; matrix products, arithmetic and copies ran while one was open for 9% of the time, Pallas kernels for 0%

profile of v1, /device:TPU:1, one launch (start us, length us, event | category | flops | bytes accessed | tf_op | source)
XLA Modules:
  0.0 535.0 jit_solution(17096273900083676755)
XLA Ops:
  7.9 1.5 copy.19
  9.4 6.1 %stack.2 = bf16[16,384,1024]{1,2,0:T(8,128)(2,1)} broadcast(bf16[384,1024]{0,1:T(8,128)(2,1)S(1)} %copy.19), dimensions={1,2} | broadcast | bytes 13369344 | tf_op jit(solution)/shard_map/stack | solution.py:122
  15.5 8.6 %all-to-all-start = ((bf16[16,384,1024]{1,2,0:T(8,128)(2,1)}), bf16[16,384,1024]{1,2,0:T(8,128)(2,1)}, u32[]{:S(2)}, u32[]{:S(2)}) async-start(bf16[16,384,1024]{1,2,0:T(8,128)(2,1)} %stack.2), calls=%async_computation | async-start | bytes 25165824 | tf_op jit(solution)/shard_map/all_to_all | solution.py:123
  24.4 197.5 %all-gather.2.cloned.1.call-done = bf16[6144,1024]{1,0:T(8,128)(2,1)} async-done(((bf16[384,1024]{1,0:T(8,128)(2,1)}), bf16[6144,1024]{1,0:T(8,128)(2,1)}) %all-gather.2.cloned.1.call-update) | async-done | bytes 12582928 | tf_op jit(solution)/shard_map/all_gather | solution.py:125
  221.8 11.9 %copy.41 = bf16[768,8,8,128]{3,2,1,0:T(8,128)(2,1)} copy(bf16[768,8,8,128]{3,1,2,0:T(8,128)(2,1)} %bitcast.92) | data formatting | bytes 25165824
  233.8 0.9 broadcast_in_dim.52.clone
  234.8 117.0 %while.20 = (s32[]{:T(128)}, f32[8,192]{1,0:T(8,128)S(1)}, f32[8,192]{1,0:T(8,128)S(1)}, f32[8,192,128]{2,1,0:T(8,128)S(1)}, f32[8,192]{1,0:T(8,128)S(1)}, /*ind...) while((s32[]{:T(128)}, f32[8,192]{1,0:T(8,128)S(1)}, ...), condition=%wide.region_9.10_spmd, body=%wide.region_0.9_spmd.sunk | while | flops 617908992 | bytes 34623504 | solution.py:158
  236.0 1.2 constant_dynamic-slice_fusion.4
  237.6 1.2 constant_dynamic-slice_fusion.5
  240.1 3.7 conditional.5
  240.9 0.9 fusion.12
  241.8 1.1 convolution_add_fusion.1
  244.9 2.8 conditional.4
  246.6 1.1 convolution_add_fusion
  249.0 1.2 constant_dynamic-slice_fusion.4
  250.6 1.2 constant_dynamic-slice_fusion.5
  253.1 3.7 conditional.5
  254.8 1.1 convolution_add_fusion.1
  257.9 2.8 conditional.4
  259.6 1.1 convolution_add_fusion
  262.0 1.2 constant_dynamic-slice_fusion.4
  263.6 1.2 constant_dynamic-slice_fusion.5
  268.5 1.2 constant_dynamic-slice_fusion.4
  270.1 1.2 constant_dynamic-slice_fusion.5
  275.0 1.2 constant_dynamic-slice_fusion.4
  276.6 1.2 constant_dynamic-slice_fusion.5
  281.5 1.2 constant_dynamic-slice_fusion.4
  283.1 1.2 constant_dynamic-slice_fusion.5
  288.0 1.2 constant_dynamic-slice_fusion.4
  289.6 1.2 constant_dynamic-slice_fusion.5
  294.5 1.2 constant_dynamic-slice_fusion.4
  296.1 1.2 constant_dynamic-slice_fusion.5
  301.0 1.2 constant_dynamic-slice_fusion.4
  302.6 1.2 constant_dynamic-slice_fusion.5
  307.5 1.2 constant_dynamic-slice_fusion.4
  309.1 1.2 constant_dynamic-slice_fusion.5
  314.0 1.2 constant_dynamic-slice_fusion.4
  315.6 1.2 constant_dynamic-slice_fusion.5
  320.5 1.2 constant_dynamic-slice_fusion.4
  322.1 1.2 constant_dynamic-slice_fusion.5
  327.0 1.2 constant_dynamic-slice_fusion.4
  328.6 1.2 constant_dynamic-slice_fusion.5
  333.5 1.2 constant_dynamic-slice_fusion.4
  335.1 1.2 constant_dynamic-slice_fusion.5
  340.0 1.2 constant_dynamic-slice_fusion.4
  341.6 1.2 constant_dynamic-slice_fusion.5
  346.5 1.2 constant_dynamic-slice_fusion.4
  348.1 1.2 constant_dynamic-slice_fusion.5
  352.1 1.4 copy_bitcast_fusion.1
  353.5 12.0 %fusion.20 = bf16[8192,384]{0,1:T(8,128)(2,1)} fusion(bf16[8192,1024]{1,0:T(8,128)(2,1)} %param.23, bf16[192,1024]{1,0:T(8,128)(2,1)S(1)} %copy_bitcast_fusion.1, bf16[192,1024]{1,0:T(8,128)(2,1)S(1)} %copy_bitcast_fusion.2), kind=kOutput, calls=%fused_computation.38 | convolution fusion | flops 6447169536 | bytes 23855104 | tf_op jit(solution)/shard_map/dot_general | solution.py:176
  365.5 1.1 copy-done.7
  368.3 8.3 %collective-permute-start = (bf16[128,1024]{0,1:T(8,128)(2,1)}, bf16[128,1024]{0,1:T(8,128)(2,1)}, u32[]{:S(2)}, u32[]{:S(2)}) collective-permute-start(bf16[128,1024]{0,1:T(8,128)(2,1)} %slice.22), channel_id=1, source_target_pairs={{0,8},{8,16},{16,24},{24,32},{32,40},{40,48},{48,56},{56,64},{64,7... | collective-permute-start | bytes 786440 | tf_op jit(solution)/shard_map/ppermute | solution.py:12
  376.8 1.2 copy.13
  378.0 1.2 iota_compare_fusion.1
  379.3 3.4 fusion.23
  382.6 2.3 fusion.26
  384.9 1.3 iota_compare_fusion
  386.2 4.7 fusion.21
  390.9 1.9 pad_maximum_fusion
  392.8 2.6 reshape_reshape.10
  395.5 4.0 add_bitcast_fusion
  401.2 1.2 copy.26
  402.4 123.5 %reduce-scatter.2.cloned.1.call-done = bf16[1024,384]{0,1:T(8,128)(2,1)} async-done(((bf16[8192,384]{0,1:T(8,128)(2,1)}), bf16[1024,384]{0,1:T(8,128)(2,1)}) %reduce-scatter.2.cloned.1.call-update) | async-done | bytes 786448 | tf_op jit(solution)/shard_map/reduce_scatter | solution.py:175
  525.9 2.3 copy.27
  (187 shorter events, 48.6 us)
Async XLA Ops:
  7.2 372.1 %copy-start = (bf16[64,128]{1,0:T(8,128)(2,1)S(1)}, bf16[64,128]{1,0:T(8,128)(2,1)}, u32[]{:S(2)}) copy-start(bf16[64,128]{1,0:T(8,128)(2,1)} %param.18) | copy-start | bytes 49156
  7.2 214.7 %all-gather.2.cloned.1.call-start = ((), (), s32[]{:S(2)}) async-start(), calls=%async_computation.2 | async-start | bytes 13369344 | tf_op jit(solution)/shard_map/all_gather | solution.py:125
  15.5 8.6 %copy-start.6 = (bf16[384,1024]{1,0:T(8,128)(2,1)S(1)}, bf16[384,1024]{1,0:T(8,128)(2,1)}, u32[]{:S(2)}) copy-start(bf16[384,1024]{1,0:T(8,128)(2,1)} %param.20) | copy-start | bytes 2359300
  15.5 218.2 %all-to-all-start = ((bf16[16,384,1024]{1,2,0:T(8,128)(2,1)}), bf16[16,384,1024]{1,2,0:T(8,128)(2,1)}, u32[]{:S(2)}, u32[]{:S(2)}) async-start(bf16[16,384,1024]{1,2,0:T(8,128)(2,1)} %stack.2), calls=%async_computation | async-start | bytes 25165824 | tf_op jit(solution)/shard_map/all_to_all | solution.py:123
  24.1 501.8 %reduce-scatter.2.cloned.1.call-start = ((), (), s32[]{:S(2)}) async-start(), calls=%async_computation.3 | async-start | bytes 7077888 | tf_op jit(solution)/shard_map/reduce_scatter | solution.py:175
  240.2 1.6 copy-start.4
  242.9 0.9 copy-start.5
  253.2 1.6 copy-start.4
  255.9 0.9 copy-start.5
  365.4 1.1 copy-start.7
  365.4 1.5 copy-start.8
  367.5 10.5 %copy-start.1 = (bf16[384,1024]{0,1:T(8,128)(2,1)}, bf16[384,1024]{0,1:T(8,128)(2,1)S(1)}, u32[]{:S(2)}) copy-start(bf16[384,1024]{0,1:T(8,128)(2,1)S(1)} %multiply_convert_fusion) | copy-start | bytes 2359300
  367.5 9.3 %copy-start.9 = (bf16[384,1024]{1,0:T(8,128)(2,1)S(1)}, bf16[384,1024]{1,0:T(8,128)(2,1)}, u32[]{:S(2)}) copy-start(bf16[384,1024]{1,0:T(8,128)(2,1)} %param.15) | copy-start | bytes 2359300
  368.3 22.7 %collective-permute-start = (bf16[128,1024]{0,1:T(8,128)(2,1)}, bf16[128,1024]{0,1:T(8,128)(2,1)}, u32[]{:S(2)}, u32[]{:S(2)}) collective-permute-start(bf16[128,1024]{0,1:T(8,128)(2,1)} %slice.22), channel_id=1, source_target_pairs={{0,8},{8,16},{16,24},{24,32},{32,40},{40,48},{48,56},{56,64},{64,7... | collective-permute-start | bytes 786440 | tf_op jit(solution)/shard_map/ppermute | solution.py:12
  386.2 4.8 slice-start
  399.4 1.1 copy-start.2
  399.5 1.4 copy-start.3
  399.5 1.4 copy-start.10
Sparse Core Ops, SparseCore 0:
  10.4 211.3 all-gather.1
  365.6 160.2 reduce-scatter.1
